TPU v7x, 256 devices: a whole 4x4x8 slice. The times are simulated.
256 devices in a mesh: cfg: 2 (over core), req: 4 (over y), seq: 32 (over z, x).
Axes of the slice: x: 4, y: 4, z: 8, core: 2. Of those that a mesh axis runs over, the one named last changes fastest.
Arguments:
- patches: float32 [16, 1024, 16], P('req', 'seq'), may hold values from -6 to 6
- noise: float32 [16, 1024, 16], P('req', 'seq'), may hold values from -6 to 6
- timesteps: int32 [16], replicated, may hold values from 50 to 950
- labels: int32 [16], replicated, may hold values from 0 to 999
- lengths: int32 [16], replicated, may hold values from 1 to 1024, 12288 in all
- time_w1: bfloat16 [256, 1152], replicated, may hold values from -0.375 to 0.375
- time_w2: bfloat16 [1152, 1152], replicated, may hold values from -0.1875 to 0.1875
- label_table: bfloat16 [1001, 1152], replicated, may hold values from -5 to 5
- patch_w: bfloat16 [16, 1152], replicated, may hold values from -1.5 to 1.5
- mod_w: bfloat16 [1152, 5760], P(None, ('req', 'seq')), may hold values from -0.1875 to 0.1875
- qkv_w: bfloat16 [1152, 3456], P('req')
- out_w: bfloat16 [1152, 1152], P(None, 'req'), may hold values from -0.1875 to 0.1875
- head_w: bfloat16 [1152, 32], replicated, may hold values from -0.1875 to 0.1875
Outputs:
- guided_update: float32 [16, 1024, 16], P('req', 'seq', 'cfg')
- hidden_norms: float32 [2, 16], P('cfg', 'req')
- max_logits: float32 [2, 16, 16], P('cfg', 'req')
Inputs may be any that keep to these rules, and one draw needn't show every extreme that they name: The lengths of the 16 requests sum to 12288, and the longest has exactly 1024 tokens.
All inputs are finite; a program needn't handle non-finite values.
Results may differ from a plain program's by a relative error of at most 0.0029.
Values may be sent and summed in bfloat16 or wider, within the bound.
A program may use at most 128 MiB of HBM per device.

v0:
```python
import math
import jax
import jax.numpy as jnp
from jax import lax
from jax.sharding import PartitionSpec as P

HEADS = 16
FREQ = 256
norm_eps = 1e-06
masked_score = -1e30
guide_scale = 4.0
plan_offset = 0.008
diffusion_steps = 1000.0


def partner(value, axis, stride):
    mask = 2**stride
    pairs = [(source, source ^ mask) for source in range(lax.axis_size(axis))]
    return lax.ppermute(value, axis, pairs)


def layer_norm(values):
    center = values - jnp.mean(values, axis=-1, keepdims=True)
    spread = jnp.mean(center * center, axis=-1, keepdims=True)
    return center * lax.rsqrt(spread + norm_eps)


def sine_table(places, count, cos_first):
    half = count // 2
    rates = jnp.exp(-math.log(10000.0) * jnp.arange(half, dtype=jnp.float32) / half)
    angles = places.astype(jnp.float32)[:, None] * rates[None, :]
    if cos_first:
        return jnp.concatenate([jnp.cos(angles), jnp.sin(angles)], axis=1)
    return jnp.concatenate([jnp.sin(angles), jnp.cos(angles)], axis=1)


def alpha_bar(steps):
    phase = (steps / diffusion_steps + plan_offset) / (1.0 + plan_offset) * (math.pi / 2.0)
    return jnp.cos(phase) ** 2


def sampler_step(patches, noise, guided, varpart, steps, valid):
    abar = alpha_bar(steps)
    abar_prev = alpha_bar(steps - 1.0)
    beta = 1.0 - abar / abar_prev
    start = (patches - jnp.sqrt(1.0 - abar) * guided) / jnp.sqrt(abar)
    mean = (
        beta * jnp.sqrt(abar_prev) / (1.0 - abar) * start
        + (1.0 - abar_prev) * jnp.sqrt(1.0 - beta) / (1.0 - abar) * patches
    )
    tilde = beta * (1.0 - abar_prev) / (1.0 - abar)
    frac = (varpart + 1.0) * 0.5
    logvar = frac * jnp.log(beta) + (1.0 - frac) * jnp.log(tilde)
    return jnp.where(valid, mean + jnp.exp(0.5 * logvar) * noise, 0.0)


def body(
    patches,
    noise,
    timesteps,
    labels,
    lengths,
    time_w1,
    time_w2,
    label_table,
    patch_w,
    mod_w,
    qkv_w,
    out_w,
    head_w,
):
    req_dev, slot_dev, patch_in = patches.shape
    width = patch_w.shape[1]
    head_dim = width // HEADS
    seq_total = slot_dev * lax.axis_size("seq")
    copy_index = lax.axis_index("cfg")
    is_cond = copy_index == 0
    tfreq = sine_table(timesteps, FREQ, True).astype(jnp.bfloat16)
    time_hidden = jax.nn.silu(jnp.dot(tfreq, time_w1, preferred_element_type=jnp.float32)).astype(
        jnp.bfloat16
    )
    time_embed = jnp.dot(time_hidden, time_w2, preferred_element_type=jnp.float32)
    label_rows = label_table.shape[0]
    label_used = jnp.where(is_cond, labels, label_rows - 1)
    one_hot = (label_used[:, None] == jnp.arange(label_rows, dtype=jnp.int32)[None, :]).astype(
        jnp.bfloat16
    )
    cond = time_embed + jnp.dot(one_hot, label_table, preferred_element_type=jnp.float32)
    cond_act = jax.nn.silu(cond).astype(jnp.bfloat16)
    mod_part = jnp.dot(cond_act, mod_w, preferred_element_type=jnp.float32)
    mod_all = lax.all_gather(mod_part, ("req", "seq"), axis=1, tiled=True)
    first_req = lax.axis_index("req") * req_dev
    modulation = lax.dynamic_slice_in_dim(mod_all, first_req, req_dev, 0).reshape(req_dev, 5, width)
    my_lengths = lax.dynamic_slice_in_dim(lengths, first_req, req_dev, 0)
    my_steps = lax.dynamic_slice_in_dim(timesteps, first_req, req_dev, 0)
    shift1 = modulation[:, 0][:, None, :]
    scale1 = modulation[:, 1][:, None, :]
    gate1 = modulation[:, 2][:, None, :]
    shift2 = modulation[:, 3][:, None, :]
    scale2 = modulation[:, 4][:, None, :]
    slot_pos = lax.axis_index("seq") * slot_dev + jnp.arange(slot_dev, dtype=jnp.int32)
    position = sine_table(slot_pos, width, False)
    token_rows = req_dev * slot_dev
    embedded = jnp.dot(
        patches.astype(jnp.bfloat16).reshape(token_rows, patch_in),
        patch_w,
        preferred_element_type=jnp.float32,
    )
    hidden0 = embedded.reshape(req_dev, slot_dev, width) + position[None, :, :]
    normed1 = (layer_norm(hidden0) * (1.0 + scale1) + shift1).astype(jnp.bfloat16)
    normed_rows = normed1.reshape(token_rows, width)
    projected = jnp.dot(
        normed_rows,
        lax.all_gather(qkv_w, "req", axis=0, tiled=True),
        preferred_element_type=jnp.float32,
    )
    query = projected[:, :width].astype(jnp.bfloat16).reshape(req_dev, slot_dev, HEADS, head_dim)
    keys_local = (
        projected[:, width : 2 * width].astype(jnp.bfloat16).reshape(req_dev, slot_dev, width)
    )
    values_local = projected[:, 2 * width :].astype(jnp.bfloat16).reshape(req_dev, slot_dev, width)
    inv_root = 1.0 / math.sqrt(head_dim)
    keys_all, values_all = (
        lax.all_gather(keys_local, "seq", axis=1, tiled=True),
        lax.all_gather(values_local, "seq", axis=1, tiled=True),
    )
    keys_heads = keys_all.reshape(req_dev, seq_total, HEADS, head_dim)
    values_heads = values_all.reshape(req_dev, seq_total, HEADS, head_dim)
    scores = (
        jnp.einsum("rqhd,rkhd->rhqk", query, keys_heads, preferred_element_type=jnp.float32)
        * inv_root
    )
    key_ok = (jnp.arange(seq_total, dtype=jnp.int32)[None, :] < my_lengths[:, None])[
        :, None, None, :
    ]
    scores = jnp.where(key_ok, scores, masked_score)
    row_max = jnp.max(scores, axis=3)
    expo = jnp.where(key_ok, jnp.exp(scores - row_max[..., None]), 0.0)
    total = jnp.sum(expo, axis=3)
    summed = jnp.einsum(
        "rhqk,rkhd->rqhd",
        expo.astype(jnp.bfloat16),
        values_heads,
        preferred_element_type=jnp.float32,
    )
    mixed = (
        (summed / jnp.transpose(total, (0, 2, 1))[..., None])
        .astype(jnp.bfloat16)
        .reshape(token_rows, width)
    )
    attended = jnp.dot(
        mixed, lax.all_gather(out_w, "req", axis=1, tiled=True), preferred_element_type=jnp.float32
    )
    hidden1 = hidden0 + gate1 * attended.reshape(req_dev, slot_dev, width)
    query_ok = slot_pos[None, :] < my_lengths[:, None]
    squares = jnp.sum(jnp.where(query_ok[:, :, None], hidden1 * hidden1, 0.0), axis=(1, 2))
    local_top = jnp.max(jnp.where(query_ok[:, None, :], row_max, masked_score), axis=2)
    total_squares = lax.psum(squares, "seq")
    top = lax.pmax(local_top, "seq")
    norm_values = jnp.sqrt(total_squares / (my_lengths.astype(jnp.float32) * width))
    normed2 = (layer_norm(hidden1) * (1.0 + scale2) + shift2).astype(jnp.bfloat16)
    prediction = jnp.dot(
        normed2.reshape(token_rows, width), head_w, preferred_element_type=jnp.float32
    ).reshape(req_dev, slot_dev, head_w.shape[1])
    other = partner(prediction, "cfg", 0)
    pred_cond = jnp.where(is_cond, prediction, other)
    pred_uncond = jnp.where(is_cond, other, prediction)
    eps_cond = pred_cond[..., :patch_in]
    eps_uncond = pred_uncond[..., :patch_in]
    guided = eps_uncond + guide_scale * (eps_cond - eps_uncond)
    varpart = pred_cond[..., patch_in:]
    channel_half = patch_in // lax.axis_size("cfg")
    channel_first = copy_index * channel_half

    def own_channels(values):
        return lax.dynamic_slice_in_dim(values, channel_first, channel_half, 2)

    steps = my_steps.astype(jnp.float32)[:, None, None]
    guided_update = sampler_step(
        own_channels(patches),
        own_channels(noise),
        own_channels(guided),
        own_channels(varpart),
        steps,
        query_ok[:, :, None],
    )
    return (guided_update, norm_values[None, :], top[None, :, :])


def solution(mesh):
    in_specs = (
        P("req", "seq", None),
        P("req", "seq", None),
        P(),
        P(),
        P(),
        P(),
        P(),
        P(),
        P(),
        P(None, ("req", "seq")),
        P("req", None),
        P(None, "req"),
        P(),
    )
    out_specs = (P("req", "seq", "cfg"), P("cfg", "req"), P("cfg", "req", None))
    return jax.shard_map(body, mesh=mesh, in_specs=in_specs, out_specs=out_specs, check_vma=False)
```

profile of v0, /device:TPU:2, one launch (start us, length us, event | category | flops | bytes accessed | tf_op | source)
XLA Modules:
  0.0 769.9 jit_solution(16310428311648811346)
XLA Ops:
  7.2 0.0 copy-start
  7.2 0.0 copy-start.4
  7.2 0.0 copy-start.5
  7.2 0.0 all-gather.6.cloned.1.call-start
  7.2 0.7 all-gather.6.cloned.1.call-update
  7.9 0.0 all-gather.10.cloned.1.call-start
  8.0 0.7 convert_element_type.45
  8.7 0.7 broadcast_select_fusion.1
  9.3 0.1 fusion.43
  9.5 0.0 copy-done
  9.5 1.7 fusion.27
  11.1 2.3 convolution_bitcast_fusion
  13.4 348.6 %all-gather = f32[128,45,16]{1,2,0:T(8,128)S(1)} all-gather(f32[1,45,16]{1,2,0:T(8,128)S(1)} %convolution_bitcast_fusion), channel_id=1, replica_groups=mesh['cfg'=2,'req'=4,'seq'=32] {'req','seq'}, dimensions={0}, use_global_device_ids=true | all-gather | bytes 371520 | tf_op jit(solution)/shard_map/all_gather | solution.py:91
  362.0 0.3 copy.24
  362.3 0.5 reshape.193
  363.0 0.4 multiply_sine_fusion
  363.3 0.1 pad_maximum_fusion
  363.4 0.0 copy-done.4
  363.4 0.0 copy-done.5
  363.4 0.3 fusion.67
  363.8 0.2 multiply_reduce_fusion.1
  364.0 0.1 slice_add_fusion
  364.1 0.2 add_convert_fusion.1
  364.3 0.0 all-gather.6.cloned.1.call-done
  364.4 0.0 copy-start.7
  364.4 0.0 copy-start.6
  364.4 4.6 convolution_convert_fusion
  369.0 0.9 fusion.65
  369.9 0.0 all-gather.10.cloned.1.call-update
  369.9 0.0 all-gather.8.cloned.1.call-start
  370.0 0.7 all-gather.8.cloned.1.call-update
  370.7 0.2 all-gather.12.cloned.1.call-start
  370.9 0.3 all-gather.12.cloned.1.call-update
  371.2 0.0 copy-done.7
  371.2 0.1 dynamic_slice.21
  371.3 0.6 copy.43
  371.9 0.1 multiply_divide_fusion.3
  372.1 0.1 broadcast_compare_fusion
  372.1 0.6 fusion.63
  372.8 0.1 iota_compare_fusion.3
  372.8 0.6 copy_bitcast_fusion
  373.5 0.9 reshape.189
  374.4 94.2 %all-gather.10.cloned.1.call-done = bf16[4,1024,1152]{2,1,0:T(8,128)(2,1)} async-done(((bf16[4,32,1152]{2,1,0:T(8,128)(2,1)}), bf16[4,1024,1152]{2,1,0:T(8,128)(2,1)}) %all-gather.10.cloned.1.call-update) | async-done | bytes 9437200 | tf_op jit(solution)/shard_map/all_gather | solution.py:124
  468.6 12.7 %copy.26 = bf16[4,1024,1152]{1,2,0:T(8,128)(2,1)} copy(bf16[4,1024,1152]{2,1,0:T(8,128)(2,1)} %all-gather.10.cloned.1.call-done) | data formatting | bytes 18874368 | tf_op jit(solution)/shard_map/all_gather | solution.py:124
  481.3 90.2 %all-gather.8.cloned.1.call-done = bf16[4,1024,1152]{2,1,0:T(8,128)(2,1)} async-done(((bf16[4,32,1152]{2,1,0:T(8,128)(2,1)}), bf16[4,1024,1152]{2,1,0:T(8,128)(2,1)}) %all-gather.8.cloned.1.call-update) | async-done | bytes 9437200 | tf_op jit(solution)/shard_map/all_gather | solution.py:125
  571.4 12.7 %copy.25 = bf16[4,1024,1152]{1,2,0:T(8,128)(2,1)} copy(bf16[4,1024,1152]{2,1,0:T(8,128)(2,1)} %all-gather.8.cloned.1.call-done) | data formatting | bytes 18874368 | tf_op jit(solution)/shard_map/all_gather | solution.py:125
  584.2 5.3 fusion
  589.5 0.0 copy-start.3
  589.5 3.2 copy-done.2
  592.7 2.4 fusion.1
  595.1 10.0 %divide_convert_fusion = bf16[4,32,16,72]{3,1,2,0:T(8,128)(2,1)} fusion(bf16[4,1024,16,72]{1,3,2,0:T(8,128)(2,1)} %bitcast.61, f32[4,16,32,1024]{3,2,1,0:T(8,128)} %copy-done.2, f32[4,16,32]{2,1,0:T(8,128)S(1)} %get-tuple-element.32, pred[4,1024]{1,0:T(4,128)(4,1)S(1)} %iota_compare_fusion.3, f32[4,32,16]{1,2,0:T(8,128)S(1)} %bitcast.66), kind=kOutput, calls=%fused_computation.20 | convolution fusion | flops 312770560 | bytes 18141184 | tf_op jit(solution)/shard_map/rhqk,rkhd->rqhd/dot_general | solution.py:140
  605.1 2.0 copy.28
  607.1 1.6 dot_general.40
  608.6 0.8 all-gather.12.cloned.1.call-done
  609.4 2.8 fusion.68
  612.2 0.3 select_reduce_fusion
  612.5 1.4 fusion.25
  613.9 0.1 collective-permute-start
  614.0 71.1 %psum.7 = f32[4]{0:T(128)S(1)} all-reduce(f32[4]{0:T(128)S(1)} %get-tuple-element.3), channel_id=1, replica_groups=mesh['cfg'=2,'req'=4,'seq'=32] {'seq'}, use_global_device_ids=true, to_apply=%region_7.8 | all-reduce | flops 4 | bytes 32 | tf_op jit(solution)/shard_map/psum | solution.py:158
  685.1 1.3 sqrt_bitcast_fusion
  686.3 0.8 select_reduce_fusion.1
  687.2 74.7 %pmax.7 = f32[1,4,16]{2,1,0:T(4,128)} all-reduce(f32[1,4,16]{2,1,0:T(4,128)S(1)} %bitcast.67), channel_id=1, replica_groups=mesh['cfg'=2,'req'=4,'seq'=32] {'seq'}, use_global_device_ids=true, to_apply=%region_9.10 | all-reduce | flops 64 | bytes 512 | tf_op jit(solution)/shard_map/pmax | solution.py:159
  761.9 0.0 collective-permute-done
  761.9 1.5 fusion.42
  (19 shorter events, 0.2 us)
Async XLA Ops:
  7.2 2.3 copy-start
  7.2 356.2 %copy-start.4 = (f32[4,32,16]{1,2,0:T(8,128)S(1)}, f32[4,32,16]{1,2,0:T(8,128)}, u32[]{:S(2)}) copy-start(f32[4,32,16]{1,2,0:T(8,128)} %param.13) | copy-start | bytes 24580
  7.2 356.2 %copy-start.5 = (bf16[16,1152]{1,0:T(8,128)(2,1)S(1)}, bf16[16,1152]{1,0:T(8,128)(2,1)}, u32[]{:S(2)}) copy-start(bf16[16,1152]{1,0:T(8,128)(2,1)} %param.21) | copy-start | bytes 110596
  7.2 357.1 %all-gather.6.cloned.1.call-start = ((), (), s32[]{:S(2)}) async-start(), calls=%async_computation | async-start | bytes 9953280 | tf_op jit(solution)/shard_map/all_gather | solution.py:114
  7.9 460.7 %all-gather.10.cloned.1.call-start = ((), (), s32[]{:S(2)}) async-start(), calls=%async_computation.2 | async-start | bytes 9732096 | tf_op jit(solution)/shard_map/all_gather | solution.py:124
  364.4 6.9 copy-start.7
  364.4 7.6 copy-start.6
  369.9 201.5 %all-gather.8.cloned.1.call-start = ((), (), s32[]{:S(2)}) async-start(), calls=%async_computation.1 | async-start | bytes 9732096 | tf_op jit(solution)/shard_map/all_gather | solution.py:125
  370.7 238.8 %all-gather.12.cloned.1.call-start = ((), (), s32[]{:S(2)}) async-start(), calls=%async_computation.3 | async-start | bytes 3317760 | tf_op jit(solution)/shard_map/all_gather | solution.py:152
  589.4 3.2 copy-start.2
  589.5 15.6 %copy-start.3 = (f32[4,16,32]{2,1,0:T(8,128)}, f32[4,16,32]{2,1,0:T(8,128)S(1)}, u32[]{:S(2)}) copy-start(f32[4,16,32]{2,1,0:T(8,128)S(1)} %get-tuple-element.32) | copy-start | bytes 24580
  595.1 168.3 %copy-start.1 = (bf16[1152,1152]{1,0:T(8,128)(2,1)S(1)}, bf16[1152,1152]{1,0:T(8,128)(2,1)}, u32[]{:S(2)}) copy-start(bf16[1152,1152]{1,0:T(8,128)(2,1)} %param.19) | copy-start | bytes 7962628
  613.9 148.0 %collective-permute-start = (f32[4,32,32]{1,2,0:T(8,128)S(1)}, f32[4,32,32]{1,2,0:T(8,128)S(1)}, u32[]{:S(2)}, u32[]{:S(2)}) collective-permute-start(f32[4,32,32]{1,2,0:T(8,128)S(1)} %fusion.25), channel_id=1, source_target_pairs={{0,128},{128,0},{1,129},{129,1},{2,130},{130,2},{3,131},{131,3},{4... | collective-permute-start | bytes 49160 | tf_op jit(solution)/shard_map/ppermute | solution.py:19
Sparse Core Ops, SparseCore 0:
  9.8 85.0 all-gather.5
  370.0 98.5 all-gather.9
  471.2 100.1 all-gather.7
  573.1 36.3 all-gather.11
where the time goes:
time: 771 us; the launch traced here: 770 us
  blocking collectives  494 us (64%)
  waiting for transfers between devices  187 us (24%)
  local copies, waits for them, and re-layouts  36.3 us (5%)
  matrix products  28.3 us (4%)
  between operations  14 us (2%)
  other arithmetic  9.52 us (1%)
    all_gather x1, blocking collectives, body(): mod_all = lax.all_gather(mod_part, ('req', 'seq'), axis=1, tiled=True)  349 us
    all_gather x1, waiting for transfers between devices, body(): lax.all_gather(keys_local, 'seq', axis=1, tiled=True)  94.2 us
    all_gather x1, waiting for transfers between devices, body(): lax.all_gather(values_local, 'seq', axis=1, tiled=True)  90.2 us
    pmax x1, blocking collectives, body(): top = lax.pmax(local_top, 'seq')  74.7 us
    psum x1, blocking collectives, body(): total_squares = lax.psum(squares, 'seq')  71.1 us
  transfers between devices with their start and end apart: 5, of which 3 were waited for; matrix products, arithmetic and copies ran while one was open for 8% of the time, Pallas kernels for 0%

commit v1 on v0

--- a/solution.py
+++ b/solution.py
@@ -120,8 +120,11 @@
     )
     values_local = projected[:, 2 * width :].astype(jnp.bfloat16).reshape(req_dev, slot_dev, width)
     inv_root = 1.0 / math.sqrt(head_dim)
+    _tell_files = lambda array_in, dim_no: jnp.concatenate(
+        lax.all_to_all(jnp.stack([array_in] * lax.psum(1, "seq")), "seq", 0, 0), axis=dim_no
+    )
     keys_all, values_all = (
-        lax.all_gather(keys_local, "seq", axis=1, tiled=True),
+        _tell_files(keys_local, 1),
         lax.all_gather(values_local, "seq", axis=1, tiled=True),
     )
     keys_heads = keys_all.reshape(req_dev, seq_total, HEADS, head_dim)

time: 771 us -> 847 us (1.099)
  local copies, waits for them, and re-layouts: 36.3 us -> 66.5 us
  starting transfers between devices: 0.43 us -> 13.4 us
  matrix products: 28.3 us -> 40.6 us
  blocking collectives: 494 us -> 504 us
  waiting for transfers between devices: 187 us -> 196 us
    all_to_all x0 -> x1, waiting for transfers between devices: none -> 194 us  [body(): lax.all_to_all(jnp.stack([array_in] * lax.psum(1, 'seq')), 'seq', 0, 0)]
    all_gather x1 -> x0, waiting for transfers between devices: 94.2 us -> none  [body(): lax.all_gather(keys_local, 'seq', axis=1, tiled=True)]
    all_gather x1, waiting for transfers between devices: 90.2 us -> 0.01 us  [body(): lax.all_gather(values_local, 'seq', axis=1, tiled=True)]
    another operation x0 -> x2, local copies, waits for them, and re-layouts: none -> 38 us  [the longest x1 33.2 us: body(): keys_heads = keys_all.reshape(req_dev, seq_total, HEADS, head_dim)]
    all_to_all x0 -> x1, starting transfers between devices: none -> 13.2 us  [body(): lax.all_to_all(jnp.stack([array_in] * lax.psum(1, 'seq')), 'seq', 0, 0)]
    all_gather x1 -> x0, local copies, waits for them, and re-layouts: 12.7 us -> none  [body(): lax.all_gather(keys_local, 'seq', axis=1, tiled=True)]
    dot_general x1, matrix products: 5.3 us -> 17.8 us  [body(): jnp.einsum('rqhd,rkhd->rhqk', query, keys_heads, preferred_element_type=j...]
    all_gather x1, blocking collectives: 349 us -> 358 us  [body(): mod_all = lax.all_gather(mod_part, ('req', 'seq'), axis=1, tiled=True)]
  transfers between devices with their start and end apart: 5 -> 5, of which waited for: 3 -> 1; matrix products, arithmetic and copies ran while one was open for 8% -> 13% of each run, Pallas kernels for 0% -> 0%
where the time goes in v1:
time: 847 us; the launch traced here: 846 us
  blocking collectives  504 us (60%)
  waiting for transfers between devices  196 us (23%)
  local copies, waits for them, and re-layouts  66.5 us (8%)
  matrix products  40.6 us (5%)
  between operations  14 us (2%)
  starting transfers between devices  13.4 us (2%)
  other arithmetic  12 us (1%)
    all_gather x1, blocking collectives, body(): mod_all = lax.all_gather(mod_part, ('req', 'seq'), axis=1, tiled=True)  358 us
    all_to_all x1, waiting for transfers between devices, body(): lax.all_to_all(jnp.stack([array_in] * lax.psum(1, 'seq')), 'seq', 0, 0)  194 us
    pmax x1, blocking collectives, body(): top = lax.pmax(local_top, 'seq')  75 us
    psum x1, blocking collectives, body(): total_squares = lax.psum(squares, 'seq')  70.9 us
    another operation x1, local copies, waits for them, and re-layouts, body(): keys_heads = keys_all.reshape(req_dev, seq_total, HEADS, head_dim)  33.2 us
    dot_general x1, matrix products, body(): jnp.einsum('rqhd,rkhd->rhqk', query, keys_heads, preferred_element_type=j...  17.8 us
  transfers between devices with their start and end apart: 5, of which 1 were waited for; matrix products, arithmetic and copies ran while one was open for 13% of the time, Pallas kernels for 0%

profile of v1, /device:TPU:2, one launch (start us, length us, event | category | flops | bytes accessed | tf_op | source)
XLA Modules:
  0.0 845.9 jit_solution(3711230394826109396)
XLA Ops:
  7.2 0.0 copy-start
  7.2 0.0 copy-start.3
  7.2 0.0 copy-start.4
  7.2 0.0 all-gather.5.cloned.1.call-start
  7.2 0.7 all-gather.5.cloned.1.call-update
  7.9 0.0 all-gather.7.cloned.1.call-start
  8.0 0.7 convert_element_type.45
  8.7 0.7 broadcast_select_fusion.1
  9.3 0.1 fusion.44
  9.5 0.0 copy-done
  9.5 1.7 fusion.28
  11.1 2.3 convolution_bitcast_fusion
  13.4 357.6 %all-gather = f32[128,45,16]{1,2,0:T(8,128)S(1)} all-gather(f32[1,45,16]{1,2,0:T(8,128)S(1)} %convolution_bitcast_fusion), channel_id=1, replica_groups=mesh['cfg'=2,'req'=4,'seq'=32] {'req','seq'}, dimensions={0}, use_global_device_ids=true | all-gather | bytes 371520 | tf_op jit(solution)/shard_map/all_gather | solution.py:91
  371.0 0.3 copy.24
  371.4 0.5 reshape.191
  372.0 0.4 multiply_sine_fusion
  372.3 0.1 pad_maximum_fusion
  372.4 0.0 copy-done.3
  372.4 0.0 copy-done.4
  372.5 0.3 fusion.68
  372.8 0.2 multiply_reduce_fusion.1
  373.0 0.1 slice_add_fusion
  373.1 0.2 add_convert_fusion.1
  373.3 0.0 all-gather.5.cloned.1.call-done
  373.4 4.6 convolution_convert_fusion
  378.0 0.8 fusion.66
  378.8 0.0 all-gather.7.cloned.1.call-update
  378.8 4.7 stack.3
  383.6 13.2 %all-to-all-start = ((bf16[32,4,32,1152]{3,2,1,0:T(8,128)(2,1)}), bf16[32,4,32,1152]{3,2,1,0:T(8,128)(2,1)}, u32[]{:S(2)}, u32[]{:S(2)}) async-start(bf16[32,4,32,1152]{3,2,1,0:T(8,128)(2,1)} %stack.3), calls=%async_computation | async-start | bytes 18874368 | tf_op jit(solution)/shard_map/all_to_all | solution.py:124
  396.8 0.0 all-gather.9.cloned.1.call-start
  396.8 0.7 all-gather.9.cloned.1.call-update
  397.5 0.0 copy-done.6
  397.5 0.1 dynamic_slice.21
  397.6 0.0 copy-done.5
  397.6 0.1 multiply_divide_fusion.3
  397.8 0.6 fusion.64
  398.4 0.6 copy_bitcast_fusion
  399.0 0.1 broadcast_compare_fusion
  399.1 0.6 copy.48
  399.7 0.1 iota_compare_fusion.3
  399.7 0.9 reshape.188
  400.7 194.3 %all-to-all-done = bf16[32,4,32,1152]{3,2,1,0:T(8,128)(2,1)} async-done(((bf16[32,4,32,1152]{3,2,1,0:T(8,128)(2,1)}), bf16[32,4,32,1152]{3,2,1,0:T(8,128)(2,1)}, u32[]{:S(2)}, u32[]{:S(2)}) %all-to-all-start) | async-done | bytes 9437216 | tf_op jit(solution)/shard_map/all_to_all | solution.py:124
  595.0 8.2 copy.26
  603.3 33.2 %reshape_reshape.3 = bf16[4,1024,16,72]{3,2,1,0:T(8,128)(2,1)} reshape(bf16[4,32,32,1152]{3,2,1,0:T(8,128)(2,1)} %copy.26) | data formatting | bytes 18874368 | tf_op jit(solution)/shard_map/reshape;reshape | solution.py:130
  636.5 12.7 %copy.25 = bf16[4,1024,1152]{1,2,0:T(8,128)(2,1)} copy(bf16[4,1024,1152]{2,1,0:T(8,128)(2,1)} %all-gather.7.cloned.1.call-done) | data formatting | bytes 18874368 | tf_op jit(solution)/shard_map/all_gather | solution.py:128
  649.2 17.8 %fusion.2 = (f32[4,16,32]{2,1,0:T(8,128)S(1)}, f32[4,16,32,1024]{3,2,1,0:T(8,128)}) fusion(pred[4,1024]{1,0:T(4,128)(4,1)S(1)} %iota_compare_fusion.3, bf16[4,1024,16,72]{3,2,1,0:T(8,128)(2,1)} %reshape_reshape.3, bf16[4,32,16,72]{3,2,1,0:T(8,128)(2,1)S(1)} %reshape.188), kind=kOutput, calls=%fused_computation.4 | convolution fusion | flops 308279296 | bytes 18132992 | tf_op jit(solution)/shard_map/rqhd,rkhd->rhqk/dot_general | solution.py:133
  666.9 4.8 fusion.3
  671.8 0.0 copy-start.1
  671.8 9.8 %divide_convert_fusion = bf16[4,32,16,72]{3,1,2,0:T(8,128)(2,1)} fusion(bf16[4,1024,16,72]{1,3,2,0:T(8,128)(2,1)} %bitcast.61, f32[4,16,32,1024]{3,2,1,0:T(8,128)} %get-tuple-element.33, f32[4,16,32]{2,1,0:T(8,128)S(1)} %get-tuple-element.32, pred[4,1024]{1,0:T(4,128)(4,1)S(1)} %iota_compare_fusion.3, f32[4,32,16]{1,2,0:T(8,128)S(1)} %bitcast.66), kind=kOutput, calls=%fused_computation.22 | convolution fusion | flops 312770560 | bytes 18141184 | tf_op jit(solution)/shard_map/rhqk,rkhd->rqhd/dot_general | solution.py:143
  681.6 0.0 copy-done.2
  681.6 2.1 copy.29
  683.7 1.5 dot_general.40
  685.3 0.0 all-gather.9.cloned.1.call-done
  685.3 2.8 fusion.69
  688.1 0.3 select_reduce_fusion
  688.3 1.4 fusion.26
  689.7 0.1 collective-permute-start
  689.8 70.9 %psum.7 = f32[4]{0:T(128)S(1)} all-reduce(f32[4]{0:T(128)S(1)} %get-tuple-element.3), channel_id=1, replica_groups=mesh['cfg'=2,'req'=4,'seq'=32] {'seq'}, use_global_device_ids=true, to_apply=%region_7.8 | all-reduce | flops 4 | bytes 32 | tf_op jit(solution)/shard_map/psum | solution.py:161
  760.7 1.3 sqrt_bitcast_fusion
  762.0 0.8 select_reduce_fusion.1
  762.8 75.0 %pmax.7 = f32[1,4,16]{2,1,0:T(4,128)} all-reduce(f32[1,4,16]{2,1,0:T(4,128)S(1)} %bitcast.67), channel_id=1, replica_groups=mesh['cfg'=2,'req'=4,'seq'=32] {'seq'}, use_global_device_ids=true, to_apply=%region_9.10 | all-reduce | flops 64 | bytes 512 | tf_op jit(solution)/shard_map/pmax | solution.py:162
  837.9 0.0 collective-permute-done
  837.9 1.5 fusion.43
  839.4 0.0 copy-done.1
  (18 shorter events, 0.1 us)
Async XLA Ops:
  7.2 2.3 copy-start
  7.2 365.3 %copy-start.3 = (f32[4,32,16]{1,2,0:T(8,128)S(1)}, f32[4,32,16]{1,2,0:T(8,128)}, u32[]{:S(2)}) copy-start(f32[4,32,16]{1,2,0:T(8,128)} %param.13) | copy-start | bytes 24580
  7.2 365.3 %copy-start.4 = (bf16[16,1152]{1,0:T(8,128)(2,1)S(1)}, bf16[16,1152]{1,0:T(8,128)(2,1)}, u32[]{:S(2)}) copy-start(bf16[16,1152]{1,0:T(8,128)(2,1)} %param.21) | copy-start | bytes 110596
  7.2 366.2 %all-gather.5.cloned.1.call-start = ((), (), s32[]{:S(2)}) async-start(), calls=%async_computation.1 | async-start | bytes 9953280 | tf_op jit(solution)/shard_map/all_gather | solution.py:114
  7.9 628.6 %all-gather.7.cloned.1.call-start = ((), (), s32[]{:S(2)}) async-start(), calls=%async_computation.2 | async-start | bytes 9732096 | tf_op jit(solution)/shard_map/all_gather | solution.py:128
  383.5 14.0 %copy-start.6 = (s32[16]{0:T(128)S(1)}, s32[16]{0:T(128)}, u32[]{:S(2)}) copy-start(s32[16]{0:T(128)} %param.17) | copy-start | bytes 196
  383.6 14.1 %copy-start.5 = (s32[16]{0:T(128)S(1)}, s32[16]{0:T(128)}, u32[]{:S(2)}) copy-start(s32[16]{0:T(128)} %param.15) | copy-start | bytes 196
  383.6 211.5 %all-to-all-start = ((bf16[32,4,32,1152]{3,2,1,0:T(8,128)(2,1)}), bf16[32,4,32,1152]{3,2,1,0:T(8,128)(2,1)}, u32[]{:S(2)}, u32[]{:S(2)}) async-start(bf16[32,4,32,1152]{3,2,1,0:T(8,128)(2,1)} %stack.3), calls=%async_computation | async-start | bytes 18874368 | tf_op jit(solution)/shard_map/all_to_all | solution.py:124
  396.8 288.5 %all-gather.9.cloned.1.call-start = ((), (), s32[]{:S(2)}) async-start(), calls=%async_computation.3 | async-start | bytes 3317760 | tf_op jit(solution)/shard_map/all_gather | solution.py:155
  666.9 14.7 %copy-start.2 = (f32[4,16,32]{2,1,0:T(8,128)}, f32[4,16,32]{2,1,0:T(8,128)S(1)}, u32[]{:S(2)}) copy-start(f32[4,16,32]{2,1,0:T(8,128)S(1)} %get-tuple-element.32) | copy-start | bytes 24580
  671.8 167.6 %copy-start.1 = (bf16[1152,1152]{1,0:T(8,128)(2,1)S(1)}, bf16[1152,1152]{1,0:T(8,128)(2,1)}, u32[]{:S(2)}) copy-start(bf16[1152,1152]{1,0:T(8,128)(2,1)} %param.19) | copy-start | bytes 7962628
  689.7 148.1 %collective-permute-start = (f32[4,32,32]{1,2,0:T(8,128)S(1)}, f32[4,32,32]{1,2,0:T(8,128)S(1)}, u32[]{:S(2)}, u32[]{:S(2)}) collective-permute-start(f32[4,32,32]{1,2,0:T(8,128)S(1)} %fusion.26), channel_id=1, source_target_pairs={{0,128},{128,0},{1,129},{129,1},{2,130},{130,2},{3,131},{131,3},{4... | collective-permute-start | bytes 49160 | tf_op jit(solution)/shard_map/ppermute | solution.py:19
Sparse Core Ops, SparseCore 0:
  9.8 85.0 all-gather.4
  378.9 207.6 all-gather.6
  588.4 37.4 all-gather.8
